TPU v7x, 32 devices: a whole 2x2x4 slice. The times are simulated.
32 devices in a mesh: rep: 2 (over core), shard: 16 (over z, y, x).
Axes of the slice: x: 2, y: 2, z: 4, core: 2. Of those that a mesh axis runs over, the one named last changes fastest.
Arguments:
- tokens: bfloat16 [12288, 1536], P(('rep', 'shard')), may hold values from -6 to 6
- prompt_ids: int32 [32, 4], P(('rep', 'shard')), may hold values from 0 to 1
- seq_offsets: int32 [32, 4], P(('rep', 'shard')), may hold values from 32 to 64, as said below
- attn_gain: bfloat16 [1536], P('shard'), may hold values from 0.5 to 1.5
- w_query: bfloat16 [1536, 1536], P('shard'), may hold values from -0.15625 to 0.15625
- w_key: bfloat16 [1536, 1536], P('shard'), may hold values from -0.15625 to 0.15625
- w_value: bfloat16 [1536, 1536], P('shard'), may hold values from -0.15625 to 0.15625
- w_outgate: bfloat16 [1536, 1536], P('shard'), may hold values from -0.15625 to 0.15625
- w_forget: bfloat16 [1536, 24], P('shard'), may hold values from -0.15625 to 0.15625
- forget_bias: bfloat16 [24], replicated, may hold values from 1 to 8
- w_output: bfloat16 [1536, 1536], P('shard'), may hold values from -0.625 to 0.625
- ffn_gain: bfloat16 [1536], P('shard'), may hold values from 0.5 to 1.5
- w_gate: bfloat16 [1536, 4096], P('shard'), may hold values from -0.15625 to 0.15625
- w_up: bfloat16 [1536, 4096], P('shard'), may hold values from -0.15625 to 0.15625
- w_down: bfloat16 [4096, 1536], P('shard'), may hold values from -0.09375 to 0.09375
- cotangent: bfloat16 [12288, 1536], P(('rep', 'shard')), may hold values from -6 to 6
Outputs:
- layer_out: bfloat16 [12288, 1536], P(('rep', 'shard'))
- tokens_grad: float32 [12288, 1536], P(('rep', 'shard'))
- attn_gain_grad: float32 [1536], P('shard')
- query_grad: float32 [1536, 1536], P('shard')
- key_grad: float32 [1536, 1536], P('shard')
- value_grad: float32 [1536, 1536], P('shard')
- outgate_grad: float32 [1536, 1536], P('shard')
- forget_grad: float32 [1536, 24], P('shard')
- forget_bias_grad: float32 [24], replicated
- output_grad: float32 [1536, 1536], P('shard')
- ffn_gain_grad: float32 [1536], P('shard')
- gate_grad: float32 [1536, 4096], P('shard')
- up_grad: float32 [1536, 4096], P('shard')
- down_grad: float32 [4096, 1536], P('shard')
Inputs may be any that keep to these rules, and one draw needn't show every extreme that they name: `prompt_ids`: each continuation follows one of the 2 prompts of its own block. `seq_offsets`: in every block at least one continuation follows its whole prompt.
All inputs are finite; a program needn't handle non-finite values.
Results may differ from a plain program's by a relative error of at most 0.023.
Values may be sent and summed in bfloat16 or wider, within the bound.
No kernel may reach another device: no remote copies, remote signals or barrier semaphores. Data moves between devices by JAX's collectives and lax.ppermute only.
A program may use at most 320 MiB of HBM per device.

v0:
```python
import jax
import jax.numpy as jnp
from jax import lax
from jax.sharding import PartitionSpec as P

PLEN = 64
CLEN = 64
NP = 2
NC = 4
EPS = 1e-06
NEGATIVE = -1e30


def chain_mask(prompt_ids, offsets):
    positions = jnp.arange(NP * PLEN + NC * CLEN, dtype=jnp.int32)
    in_prompt = positions < NP * PLEN
    after_prompts = positions - NP * PLEN
    sequence = jnp.where(in_prompt, positions // PLEN, NP + after_prompts // CLEN)
    within = jnp.where(in_prompt, positions % PLEN, after_prompts % CLEN)
    cont_index = sequence - NP
    selector = (cont_index[:, None] == jnp.arange(NC, dtype=jnp.int32)[None, :]).astype(jnp.int32)
    owner_id = jnp.where(in_prompt, -1, jnp.sum(selector * prompt_ids[None, :], axis=1))
    reach_end = jnp.sum(selector * offsets[None, :], axis=1)
    same_seq = (sequence[:, None] == sequence[None, :]) & (within[None, :] <= within[:, None])
    from_prompt = (owner_id[:, None] == sequence[None, :]) & (within[None, :] < reach_end[:, None])
    return same_seq | from_prompt


def normalize(values):
    inverse = lax.rsqrt(jnp.mean(values * values, axis=1, keepdims=True) + EPS)
    return (values * inverse, inverse)


def norm_back(grad_scaled, scaled, inverse):
    return inverse * (grad_scaled - scaled * jnp.mean(grad_scaled * scaled, axis=1, keepdims=True))


def matmul(left_side, right_side):
    return jnp.dot(left_side, right_side, preferred_element_type=jnp.float32)


def matmul_tn(left_side, right_side):
    return lax.dot_general(
        left_side, right_side, (((0,), (0,)), ((), ())), preferred_element_type=jnp.float32
    )


def matmul_nt(left_side, right_side):
    return lax.dot_general(
        left_side, right_side, (((1,), (1,)), ((), ())), preferred_element_type=jnp.float32
    )


def decayed_scores(query_low, key_low, decay_sum, chain_ok, score_scale):
    logits = jnp.einsum("qhd,khd->hqk", query_low, key_low, preferred_element_type=jnp.float32)
    decay_t = decay_sum.T
    logits = logits * score_scale + decay_t[:, :, None] - decay_t[:, None, :]
    return jnp.where(chain_ok[None, :, :], logits, NEGATIVE)


def local(
    tokens,
    prompt_ids,
    seq_offsets,
    attn_gain,
    w_query,
    w_key,
    w_value,
    w_outgate,
    w_forget,
    forget_bias,
    w_output,
    ffn_gain,
    w_gate,
    w_up,
    w_down,
    cotangent,
):
    row_count = tokens.shape[0]
    model_width = tokens.shape[1]
    head_count = w_forget.shape[1]
    head_dim = model_width // head_count
    score_scale = head_dim ** (-0.5)
    chain_ok = chain_mask(prompt_ids[0], seq_offsets[0])
    chain_float = chain_ok.astype(jnp.float32)
    inputs = tokens.astype(jnp.float32)
    scaled1, inverse1 = normalize(inputs)
    gain_part = lax.all_gather(attn_gain, "shard", axis=0, tiled=True)
    query_part = lax.all_gather(w_query, "shard", axis=0, tiled=True)
    key_part = lax.all_gather(w_key, "shard", axis=0, tiled=True)
    value_part = lax.all_gather(w_value, "shard", axis=0, tiled=True)
    outgate_part = lax.all_gather(w_outgate, "shard", axis=0, tiled=True)
    forget_part = lax.all_gather(w_forget, "shard", axis=0, tiled=True)
    normed_part = (scaled1 * gain_part.astype(jnp.float32)).astype(jnp.bfloat16)
    gain_one = gain_part
    normed1 = normed_part
    query_proj = matmul(normed_part, query_part)
    key_proj = matmul(normed_part, key_part)
    value_proj = matmul(normed_part, value_part)
    outgate_pre = matmul(normed_part, outgate_part)
    forget_pre = matmul(normed_part, forget_part)
    query_low = query_proj.astype(jnp.bfloat16).reshape(row_count, head_count, head_dim)
    key_low = key_proj.astype(jnp.bfloat16).reshape(row_count, head_count, head_dim)
    value_low = value_proj.astype(jnp.bfloat16).reshape(row_count, head_count, head_dim)
    forget_in = forget_pre + forget_bias.astype(jnp.float32)[None, :]
    decay_sum = jnp.dot(chain_float, jax.nn.log_sigmoid(forget_in), precision=lax.Precision.HIGHEST)
    logits = decayed_scores(query_low, key_low, decay_sum, chain_ok, score_scale)
    top_score = jnp.max(logits, axis=2, keepdims=True)
    exp_scores = jnp.exp(logits - top_score)
    denominator = jnp.sum(exp_scores, axis=2, keepdims=True)
    log_total = top_score + jnp.log(denominator)
    probs_low = (exp_scores / denominator).astype(jnp.bfloat16)
    attended = jnp.einsum(
        "hqk,khd->qhd", probs_low, value_low, preferred_element_type=jnp.float32
    ).reshape(row_count, model_width)
    gate_open = jax.nn.sigmoid(outgate_pre)
    gated_low = (attended * gate_open).astype(jnp.bfloat16)
    branch_attn = matmul(gated_low, lax.all_gather(w_output, "shard", axis=0, tiled=True))
    residual = inputs + branch_attn
    scaled2, inverse2 = normalize(residual)
    gain_part = lax.all_gather(ffn_gain, "shard", axis=0, tiled=True)
    gate_part = lax.all_gather(w_gate, "shard", axis=0, tiled=True)
    up_part = lax.all_gather(w_up, "shard", axis=0, tiled=True)
    normed_part = (scaled2 * gain_part.astype(jnp.float32)).astype(jnp.bfloat16)
    gate_pre = matmul(normed_part, gate_part)
    up_pre = matmul(normed_part, up_part)
    sig_gate = jax.nn.sigmoid(gate_pre)
    silu_gate = gate_pre * sig_gate
    act_low = (silu_gate * up_pre).astype(jnp.bfloat16)
    branch_ffn = matmul(act_low, lax.all_gather(w_down, "shard", axis=0, tiled=True))
    layer_out = (residual + branch_ffn).astype(jnp.bfloat16)
    grad_out = cotangent.astype(jnp.float32)
    grad_act = matmul_nt(cotangent, lax.all_gather(w_down, "shard", axis=0, tiled=True))
    grad_gate = (grad_act * up_pre * sig_gate * (1.0 + gate_pre * (1.0 - sig_gate))).astype(
        jnp.bfloat16
    )
    grad_up = (grad_act * silu_gate).astype(jnp.bfloat16)
    gate_part = lax.all_gather(w_gate, "shard", axis=0, tiled=True)
    up_part = lax.all_gather(w_up, "shard", axis=0, tiled=True)
    contribution = matmul_nt(grad_gate, gate_part) + matmul_nt(grad_up, up_part)
    grad_normed2 = contribution
    grad_down = matmul_tn(act_low, cotangent)
    grad_gate_w = matmul_tn(normed_part, grad_gate)
    grad_up_w = matmul_tn(normed_part, grad_up)
    grad_gain2 = jnp.sum(grad_normed2 * scaled2, axis=0)
    ffn_parts = (
        lax.psum_scatter(
            grad_gain2.astype(jnp.bfloat16), "shard", scatter_dimension=0, tiled=True
        ).astype(jnp.float32),
        lax.psum_scatter(
            grad_gate_w.astype(jnp.bfloat16), "shard", scatter_dimension=0, tiled=True
        ).astype(jnp.float32),
        lax.psum_scatter(
            grad_up_w.astype(jnp.bfloat16), "shard", scatter_dimension=0, tiled=True
        ).astype(jnp.float32),
        lax.psum_scatter(
            grad_down.astype(jnp.bfloat16), "shard", scatter_dimension=0, tiled=True
        ).astype(jnp.float32),
    )
    grad_resid = grad_out + norm_back(
        grad_normed2 * gain_part.astype(jnp.float32), scaled2, inverse2
    )
    grad_attn = grad_resid.astype(jnp.bfloat16)
    grad_gated = matmul_nt(grad_attn, lax.all_gather(w_output, "shard", axis=0, tiled=True))
    grad_output_w = matmul_tn(gated_low, grad_attn)
    grad_attended = (
        (grad_gated * gate_open).astype(jnp.bfloat16).reshape(row_count, head_count, head_dim)
    )
    grad_outgate = (grad_gated * attended * gate_open * (1.0 - gate_open)).astype(jnp.bfloat16)
    logits = decayed_scores(query_low, key_low, decay_sum, chain_ok, score_scale)
    prob_full = jnp.exp(logits - log_total)
    prob_again = prob_full.astype(jnp.bfloat16)
    grad_probs = jnp.einsum(
        "qhd,khd->hqk", grad_attended, value_low, preferred_element_type=jnp.float32
    )
    grad_value = jnp.einsum(
        "hqk,qhd->khd", prob_again, grad_attended, preferred_element_type=jnp.float32
    )
    grad_logits = prob_full * (grad_probs - jnp.sum(prob_full * grad_probs, axis=2, keepdims=True))
    grad_qk = (grad_logits * score_scale).astype(jnp.bfloat16)
    grad_query = jnp.einsum("hqk,khd->qhd", grad_qk, key_low, preferred_element_type=jnp.float32)
    grad_key = jnp.einsum("hqk,qhd->khd", grad_qk, query_low, preferred_element_type=jnp.float32)
    grad_decay = (jnp.sum(grad_logits, axis=2) - jnp.sum(grad_logits, axis=1)).T
    grad_log_forget = lax.dot_general(
        chain_float, grad_decay, (((0,), (0,)), ((), ())), precision=lax.Precision.HIGHEST
    )
    grad_forget_in = grad_log_forget * jax.nn.sigmoid(-forget_in)
    grad_bias = lax.psum(jnp.sum(grad_forget_in, axis=0), ("rep", "shard"))
    grad_query_low = grad_query.reshape(row_count, model_width).astype(jnp.bfloat16)
    grad_key_low = grad_key.reshape(row_count, model_width).astype(jnp.bfloat16)
    grad_value_low = grad_value.reshape(row_count, model_width).astype(jnp.bfloat16)
    grad_forget_low = grad_forget_in.astype(jnp.bfloat16)
    query_part = lax.all_gather(w_query, "shard", axis=0, tiled=True)
    key_part = lax.all_gather(w_key, "shard", axis=0, tiled=True)
    value_part = lax.all_gather(w_value, "shard", axis=0, tiled=True)
    outgate_part = lax.all_gather(w_outgate, "shard", axis=0, tiled=True)
    forget_part = lax.all_gather(w_forget, "shard", axis=0, tiled=True)
    contribution = (
        matmul_nt(grad_query_low, query_part)
        + matmul_nt(grad_key_low, key_part)
        + matmul_nt(grad_value_low, value_part)
        + matmul_nt(grad_outgate, outgate_part)
        + matmul_nt(grad_forget_low, forget_part)
    )
    grad_query_w = matmul_tn(normed1, grad_query_low)
    grad_key_w = matmul_tn(normed1, grad_key_low)
    grad_value_w = matmul_tn(normed1, grad_value_low)
    grad_outgate_w = matmul_tn(normed1, grad_outgate)
    grad_forget_w = matmul_tn(normed1, grad_forget_low)
    grad_gain1 = jnp.sum(contribution * scaled1, axis=0)
    grad_inputs = grad_resid + norm_back(
        contribution * gain_one.astype(jnp.float32), scaled1, inverse1
    )
    attn_parts = (
        lax.psum_scatter(
            grad_gain1.astype(jnp.bfloat16), "shard", scatter_dimension=0, tiled=True
        ).astype(jnp.float32),
        lax.psum_scatter(
            grad_query_w.astype(jnp.bfloat16), "shard", scatter_dimension=0, tiled=True
        ).astype(jnp.float32),
        lax.psum_scatter(
            grad_key_w.astype(jnp.bfloat16), "shard", scatter_dimension=0, tiled=True
        ).astype(jnp.float32),
        lax.psum_scatter(
            grad_value_w.astype(jnp.bfloat16), "shard", scatter_dimension=0, tiled=True
        ).astype(jnp.float32),
        lax.psum_scatter(
            grad_outgate_w.astype(jnp.bfloat16), "shard", scatter_dimension=0, tiled=True
        ).astype(jnp.float32),
        lax.psum_scatter(
            grad_forget_w.astype(jnp.bfloat16), "shard", scatter_dimension=0, tiled=True
        ).astype(jnp.float32),
        lax.psum_scatter(
            grad_output_w.astype(jnp.bfloat16), "shard", scatter_dimension=0, tiled=True
        ).astype(jnp.float32),
    )
    summed = (
        lax.psum(attn_parts[0].astype(jnp.bfloat16), "rep").astype(jnp.float32),
        lax.psum(attn_parts[1].astype(jnp.bfloat16), "rep").astype(jnp.float32),
        lax.psum(attn_parts[2].astype(jnp.bfloat16), "rep").astype(jnp.float32),
        lax.psum(attn_parts[3].astype(jnp.bfloat16), "rep").astype(jnp.float32),
        lax.psum(attn_parts[4].astype(jnp.bfloat16), "rep").astype(jnp.float32),
        lax.psum(attn_parts[5].astype(jnp.bfloat16), "rep").astype(jnp.float32),
        lax.psum(attn_parts[6].astype(jnp.bfloat16), "rep").astype(jnp.float32),
        lax.psum(ffn_parts[0].astype(jnp.bfloat16), "rep").astype(jnp.float32),
        lax.psum(ffn_parts[1].astype(jnp.bfloat16), "rep").astype(jnp.float32),
        lax.psum(ffn_parts[2].astype(jnp.bfloat16), "rep").astype(jnp.float32),
        lax.psum(ffn_parts[3].astype(jnp.bfloat16), "rep").astype(jnp.float32),
    )
    return (
        layer_out,
        grad_inputs,
        summed[0],
        summed[1],
        summed[2],
        summed[3],
        summed[4],
        summed[5],
        grad_bias,
        summed[6],
        summed[7],
        summed[8],
        summed[9],
        summed[10],
    )


def solution(mesh):
    in_specs = (
        P(("rep", "shard"), None),
        P(("rep", "shard"), None),
        P(("rep", "shard"), None),
        P("shard"),
        P("shard", None),
        P("shard", None),
        P("shard", None),
        P("shard", None),
        P("shard", None),
        P(),
        P("shard", None),
        P("shard"),
        P("shard", None),
        P("shard", None),
        P("shard", None),
        P(("rep", "shard"), None),
    )
    out_specs = (
        P(("rep", "shard"), None),
        P(("rep", "shard"), None),
        P("shard"),
        P("shard", None),
        P("shard", None),
        P("shard", None),
        P("shard", None),
        P("shard", None),
        P(),
        P("shard", None),
        P("shard"),
        P("shard", None),
        P("shard", None),
        P("shard", None),
    )
    return jax.shard_map(local, mesh=mesh, in_specs=in_specs, out_specs=out_specs, check_vma=False)
```

profile of v0, /device:TPU:0, one launch (start us, length us, event | category | flops | bytes accessed | tf_op | source)
XLA Modules:
  0.0 2422.7 jit_solution(16868182657455146212)
XLA Ops:
  14.6 45.2 %all-reduce.5 = (bf16[1536]{0:T(1024)(128)(2,1)S(1)}, bf16[1536]{0:T(1024)(128)(2,1)S(1)}) all-reduce(bf16[1536]{0:T(1024)(128)(2,1)S(1)} %dynamic-update-slice, bf16[1536]{0:T(1024)(128)(2,1)S(1)} %dynamic-update-slice.1), channel_id=1, replica_groups=mesh['rep'=2,'shard'=16] {'shard'}, use_global_device_ids=true, to_apply=%add | all-reduce | flops 3072 | bytes 12288
  59.8 37.5 %all-gather = bf16[16,96,24]{1,2,0:T(8,128)(2,1)S(1)} all-gather(bf16[1,96,24]{1,2,0:T(8,128)(2,1)S(1)} %bitcast.93), channel_id=1, replica_groups=mesh['rep'=2,'shard'=16] {'shard'}, dimensions={0}, use_global_device_ids=true | all-gather | bytes 78336 | tf_op jit(solution)/shard_map/all_gather | solution.py:93
  105.3 71.1 %all-gather.14.cloned.1.call-done = bf16[1536,1536]{1,0:T(8,128)(2,1)} async-done(((bf16[96,1536]{1,0:T(8,128)(2,1)}), bf16[1536,1536]{1,0:T(8,128)(2,1)}) %all-gather.14.cloned.1.call-update) | async-done | bytes 4718608 | tf_op jit(solution)/shard_map/all_gather | solution.py:90
  176.4 5.4 convolution_convert_fusion.8
  183.5 74.1 %all-gather.10.cloned.1.call-done = bf16[1536,1536]{1,0:T(8,128)(2,1)} async-done(((bf16[96,1536]{1,0:T(8,128)(2,1)}), bf16[1536,1536]{1,0:T(8,128)(2,1)}) %all-gather.10.cloned.1.call-update) | async-done | bytes 4718608 | tf_op jit(solution)/shard_map/all_gather | solution.py:91
  257.6 5.4 convolution_convert_fusion.10
  265.4 7.8 fusion.85
  273.2 7.4 fusion.4
  280.6 9.0 fusion.10
  292.0 46.6 %all-gather.16.cloned.1.call-done = bf16[1536,1536]{1,0:T(8,128)(2,1)} async-done(((bf16[96,1536]{1,0:T(8,128)(2,1)}), bf16[1536,1536]{1,0:T(8,128)(2,1)}) %all-gather.16.cloned.1.call-update) | async-done | bytes 4718608 | tf_op jit(solution)/shard_map/all_gather | solution.py:92
  338.6 6.4 multiply_convert_fusion.9
  345.1 74.6 %all-gather.18.cloned.1.call-done = bf16[1536,1536]{1,0:T(8,128)(2,1)} async-done(((bf16[96,1536]{1,0:T(8,128)(2,1)}), bf16[1536,1536]{1,0:T(8,128)(2,1)}) %all-gather.18.cloned.1.call-update) | async-done | bytes 4718608 | tf_op jit(solution)/shard_map/all_gather | solution.py:118
  419.6 4.8 multiply_reduce_fusion.3
  426.4 146.0 %all-gather.22.cloned.1.call-done = bf16[1536,4096]{1,0:T(8,128)(2,1)} async-done(((bf16[96,4096]{1,0:T(8,128)(2,1)}), bf16[1536,4096]{1,0:T(8,128)(2,1)}) %all-gather.22.cloned.1.call-update) | async-done | bytes 12582928 | tf_op jit(solution)/shard_map/all_gather | solution.py:123
  572.4 9.9 fusion.88
  582.3 142.5 %all-gather.20.cloned.1.call-done = bf16[1536,4096]{1,0:T(8,128)(2,1)} async-done(((bf16[96,4096]{1,0:T(8,128)(2,1)}), bf16[1536,4096]{1,0:T(8,128)(2,1)}) %all-gather.20.cloned.1.call-update) | async-done | bytes 12582928 | tf_op jit(solution)/shard_map/all_gather | solution.py:122
  724.8 9.9 fusion.87
  734.7 142.5 %all-gather.24.cloned.1.call-done = bf16[4096,1536]{1,0:T(8,128)(2,1)} async-done(((bf16[256,1536]{1,0:T(8,128)(2,1)}), bf16[4096,1536]{1,0:T(8,128)(2,1)}) %all-gather.24.cloned.1.call-update) | async-done | bytes 12582928 | tf_op jit(solution)/shard_map/all_gather | solution.py:130
  877.2 15.0 multiply_convert_fusion.1
  892.2 9.7 fusion.89
  902.0 9.3 multiply_reduce_fusion.1
  918.2 6.9 multiply_convert_fusion.6
  934.6 8.2 fusion.31
  943.8 4.5 convolution_convert_fusion.5
  948.4 22.3 fusion.83
  970.7 8.2 fusion.30
  979.9 4.5 convolution_convert_fusion.6
  984.5 6.6 fusion.29
  992.2 4.8 convolution_convert_fusion.7
  997.1 11.3 convolution_convert_fusion
  1008.5 11.3 convolution_convert_fusion.1
  1020.0 11.4 convolution_convert_fusion.2
  1037.3 4.8 fusion.90
  1042.2 5.9 convolution_add_fusion.3
  1048.1 38.9 %psum.90 = f32[24]{0:T(128)} all-reduce(f32[24]{0:T(128)S(1)} %get-tuple-element.53), channel_id=1, replica_groups=mesh['rep'=2,'shard'=16] {'rep','shard'}, use_global_device_ids=true, to_apply=%region_25.26 | all-reduce | flops 24 | bytes 192 | tf_op jit(solution)/shard_map/psum | solution.py:188
  1086.9 110.5 %reduce-scatter.18.cloned.1.call-done = bf16[96,1536]{1,0:T(8,128)(2,1)} async-done(((bf16[1536,1536]{1,0:T(8,128)(2,1)}), bf16[96,1536]{1,0:T(8,128)(2,1)}) %reduce-scatter.18.cloned.1.call-update) | async-done | bytes 294928 | tf_op jit(solution)/shard_map/reduce_scatter | solution.py:227
  1197.4 143.3 %reduce-scatter.16.cloned.1.call-done = bf16[96,1536]{1,0:T(8,128)(2,1)} async-done(((bf16[1536,1536]{1,0:T(8,128)(2,1)}), bf16[96,1536]{1,0:T(8,128)(2,1)}) %reduce-scatter.16.cloned.1.call-update) | async-done | bytes 294928 | tf_op jit(solution)/shard_map/reduce_scatter | solution.py:224
  1340.7 142.9 %reduce-scatter.14.cloned.1.call-done = bf16[96,1536]{1,0:T(8,128)(2,1)} async-done(((bf16[1536,1536]{1,0:T(8,128)(2,1)}), bf16[96,1536]{1,0:T(8,128)(2,1)}) %reduce-scatter.14.cloned.1.call-update) | async-done | bytes 294928 | tf_op jit(solution)/shard_map/reduce_scatter | solution.py:221
  1483.7 143.1 %reduce-scatter.12.cloned.1.call-done = bf16[96,1536]{1,0:T(8,128)(2,1)} async-done(((bf16[1536,1536]{1,0:T(8,128)(2,1)}), bf16[96,1536]{1,0:T(8,128)(2,1)}) %reduce-scatter.12.cloned.1.call-update) | async-done | bytes 294928 | tf_op jit(solution)/shard_map/reduce_scatter | solution.py:218
  1626.7 207.2 %reduce-scatter.26.cloned.1.call-done = bf16[256,1536]{1,0:T(8,128)(2,1)} async-done(((bf16[4096,1536]{1,0:T(8,128)(2,1)}), bf16[256,1536]{1,0:T(8,128)(2,1)}) %reduce-scatter.26.cloned.1.call-update) | async-done | bytes 786448 | tf_op jit(solution)/shard_map/reduce_scatter | solution.py:156
  1834.0 207.7 %reduce-scatter.24.cloned.1.call-done = bf16[96,4096]{1,0:T(8,128)(2,1)} async-done(((bf16[1536,4096]{1,0:T(8,128)(2,1)}), bf16[96,4096]{1,0:T(8,128)(2,1)}) %reduce-scatter.24.cloned.1.call-update) | async-done | bytes 786448 | tf_op jit(solution)/shard_map/reduce_scatter | solution.py:153
  2041.7 207.7 %reduce-scatter.22.cloned.1.call-done = bf16[96,4096]{1,0:T(8,128)(2,1)} async-done(((bf16[1536,4096]{1,0:T(8,128)(2,1)}), bf16[96,4096]{1,0:T(8,128)(2,1)}) %reduce-scatter.22.cloned.1.call-update) | async-done | bytes 786448 | tf_op jit(solution)/shard_map/reduce_scatter | solution.py:150
  2249.4 5.6 convolution_add_fusion.2
  2255.1 4.5 convolution_add_fusion.1
  2262.4 41.8 %all-reduce.4 = (bf16[1536]{0:T(1024)(128)(2,1)}, bf16[1536]{0:T(1024)(128)(2,1)}) all-reduce(bf16[1536]{0:T(1024)(128)(2,1)S(1)} %get-tuple-element.18, bf16[1536]{0:T(1024)(128)(2,1)} %get-tuple-element.16), channel_id=2, replica_groups=mesh['rep'=2,'shard'=16] {'shard'}, use_global_device_ids=true, to_apply=%region_12.13.clone | all-reduce | flops 3072 | bytes 12288
  2310.8 9.3 fusion.19
  2320.1 56.9 %reduce-scatter.28.cloned.1.call-done = bf16[96,24]{1,0:T(8,128)(2,1)} async-done(((bf16[1536,24]{1,0:T(8,128)(2,1)}), bf16[96,24]{1,0:T(8,128)(2,1)}) %reduce-scatter.28.cloned.1.call-update) | async-done | bytes 4624
  2382.0 22.1 all-reduce.10.cloned.1.call-done
  (175 shorter events, 73.3 us)
Async XLA Ops:
  7.2 5.6 copy-start.31
  7.2 5.6 copy-start.35
  7.2 6.9 copy-start.36
  7.2 7.1 copy-start.37
  7.2 52.6 %copy-start.30 = (bf16[96,24]{0,1:T(8,128)(2,1)S(1)}, bf16[96,24]{0,1:T(8,128)(2,1)}, u32[]{:S(2)}) copy-start(bf16[96,24]{0,1:T(8,128)(2,1)} %param.24) | copy-start | bytes 13828
  7.2 90.3 %copy-start.33 = (s32[1,4]{1,0:T(1,128)S(1)}, s32[1,4]{1,0:T(1,128)}, u32[]{:S(2)}) copy-start(s32[1,4]{1,0:T(1,128)} %param.18) | copy-start | bytes 52
  7.2 90.3 %copy-start.32 = (s32[1,4]{1,0:T(1,128)S(1)}, s32[1,4]{1,0:T(1,128)}, u32[]{:S(2)}) copy-start(s32[1,4]{1,0:T(1,128)} %param.17) | copy-start | bytes 52
  7.3 90.4 %copy-start = (bf16[384,1536]{1,0:T(8,128)(2,1)S(1)}, bf16[384,1536]{1,0:T(8,128)(2,1)}, u32[]{:S(2)}) copy-start(bf16[384,1536]{1,0:T(8,128)(2,1)} %param.16) | copy-start | bytes 3538948
  7.3 92.6 %all-gather.12.cloned.1.call-start = ((), (), s32[]{:S(2)}) async-start(), calls=%async_computation.10 | async-start | bytes 5013504 | tf_op jit(solution)/shard_map/all_gather | solution.py:89
  8.0 168.4 %all-gather.14.cloned.1.call-start = ((), (), s32[]{:S(2)}) async-start(), calls=%async_computation.11 | async-start | bytes 5013504 | tf_op jit(solution)/shard_map/all_gather | solution.py:90
  8.7 248.8 %all-gather.10.cloned.1.call-start = ((), (), s32[]{:S(2)}) async-start(), calls=%async_computation.9 | async-start | bytes 5013504 | tf_op jit(solution)/shard_map/all_gather | solution.py:91
  9.5 329.1 %all-gather.16.cloned.1.call-start = ((), (), s32[]{:S(2)}) async-start(), calls=%async_computation.12 | async-start | bytes 5013504 | tf_op jit(solution)/shard_map/all_gather | solution.py:92
  10.1 409.6 %all-gather.18.cloned.1.call-start = ((), (), s32[]{:S(2)}) async-start(), calls=%async_computation.13 | async-start | bytes 5013504 | tf_op jit(solution)/shard_map/all_gather | solution.py:118
  10.6 561.7 %all-gather.22.cloned.1.call-start = ((), (), s32[]{:S(2)}) async-start(), calls=%async_computation.15 | async-start | bytes 13369344 | tf_op jit(solution)/shard_map/all_gather | solution.py:123
  11.2 713.6 %all-gather.20.cloned.1.call-start = ((), (), s32[]{:S(2)}) async-start(), calls=%async_computation.14 | async-start | bytes 13369344 | tf_op jit(solution)/shard_map/all_gather | solution.py:122
  12.0 865.2 %all-gather.24.cloned.1.call-start = ((), (), s32[]{:S(2)}) async-start(), calls=%async_computation.16 | async-start | bytes 13369344 | tf_op jit(solution)/shard_map/all_gather | solution.py:130
  12.7 1074.2 %reduce-scatter.20.cloned.1.call-start = ((), (), s32[]{:S(2)}) async-start(), calls=%async_computation.21 | async-start | bytes 5013504 | tf_op jit(solution)/shard_map/reduce_scatter | solution.py:233
  105.2 160.1 %copy-start.5 = (bf16[384,1536]{0,1:T(8,128)(2,1)}, bf16[384,1536]{0,1:T(8,128)(2,1)S(1)}, u32[]{:S(2)}) copy-start(bf16[384,1536]{0,1:T(8,128)(2,1)S(1)} %copy.67) | copy-start | bytes 3538948
  183.5 81.9 %copy-start.4 = (bf16[384,1536]{0,1:T(8,128)(2,1)}, bf16[384,1536]{0,1:T(8,128)(2,1)S(1)}, u32[]{:S(2)}) copy-start(bf16[384,1536]{0,1:T(8,128)(2,1)S(1)} %copy.68) | copy-start | bytes 3538948
  273.2 7.5 copy-start.21
  273.2 7.5 copy-start.13
  280.6 9.1 copy-start.22
  292.0 53.1 %copy-start.1 = (f32[384,1536]{1,0:T(8,128)}, f32[384,1536]{1,0:T(8,128)S(1)}, u32[]{:S(2)}) copy-start(f32[384,1536]{1,0:T(8,128)S(1)} %copy.71) | copy-start | bytes 7077892
  424.4 477.5 %copy-start.2 = (f32[384,1536]{1,0:T(8,128)}, f32[384,1536]{1,0:T(8,128)S(1)}, u32[]{:S(2)}) copy-start(f32[384,1536]{1,0:T(8,128)S(1)} %get-tuple-element.49) | copy-start | bytes 7077892
  892.2 9.8 copy-start.29
  892.2 9.8 copy-start.40
  902.0 9.3 copy-start.6
  918.1 279.3 %reduce-scatter.18.cloned.1.call-start = ((), (), s32[]{:S(2)}) async-start(), calls=%async_computation.20 | async-start | bytes 5013504 | tf_op jit(solution)/shard_map/reduce_scatter | solution.py:227
  918.2 7.9 copy-start.27
  930.6 410.2 %reduce-scatter.16.cloned.1.call-start = ((), (), s32[]{:S(2)}) async-start(), calls=%async_computation.19 | async-start | bytes 5013504 | tf_op jit(solution)/shard_map/reduce_scatter | solution.py:224
  948.4 535.3 %reduce-scatter.14.cloned.1.call-start = ((), (), s32[]{:S(2)}) async-start(), calls=%async_computation.18 | async-start | bytes 5013504 | tf_op jit(solution)/shard_map/reduce_scatter | solution.py:221
  984.5 642.2 %reduce-scatter.12.cloned.1.call-start = ((), (), s32[]{:S(2)}) async-start(), calls=%async_computation.17 | async-start | bytes 5013504 | tf_op jit(solution)/shard_map/reduce_scatter | solution.py:218
  997.1 836.9 %reduce-scatter.26.cloned.1.call-start = ((), (), s32[]{:S(2)}) async-start(), calls=%async_computation.24 | async-start | bytes 13369344 | tf_op jit(solution)/shard_map/reduce_scatter | solution.py:156
  1008.5 1033.2 %reduce-scatter.24.cloned.1.call-start = ((), (), s32[]{:S(2)}) async-start(), calls=%async_computation.23 | async-start | bytes 13369344 | tf_op jit(solution)/shard_map/reduce_scatter | solution.py:153
  1019.9 1229.5 %reduce-scatter.22.cloned.1.call-start = ((), (), s32[]{:S(2)}) async-start(), calls=%async_computation.22 | async-start | bytes 13369344 | tf_op jit(solution)/shard_map/reduce_scatter | solution.py:150
  1031.4 1345.7 %reduce-scatter.28.cloned.1.call-start = ((), (), s32[]{:S(2)}) async-start(), calls=%async_computation.25 | async-start | bytes 417792
  1037.0 1367.0 %all-reduce.10.cloned.1.call-start = ((), (), s32[]{:S(2)}) async-start(), calls=%async_computation.26 | async-start | bytes 7667712 | tf_op jit(solution)/shard_map/psum | solution.py:239
  1037.3 4.9 copy-start.11
  2249.4 5.6 copy-start.8
  2255.0 4.5 copy-start.20
  2255.0 4.5 copy-start.25
  2306.9 3.8 copy-start.3
  2306.9 3.8 copy-start.41
  2310.7 67.1 %copy-start.34 = (bf16[96]{0:T(256)(128)(2,1)S(1)}, bf16[96]{0:T(256)(128)(2,1)}, u32[]{:S(2)}) copy-start(bf16[96]{0:T(256)(128)(2,1)} %dynamic-slice.5) | copy-start | bytes 580
  2404.0 5.7 copy-start.18
  2404.0 6.5 copy-start.17
  2404.0 7.4 copy-start.16
  2407.8 4.9 copy-start.15
  (12 other events, 16.3 us)
Sparse Core Ops, SparseCore 0:
  10.9 83.8 all-gather.11
  97.6 78.7 all-gather.13
  179.2 78.3 all-gather.9
  260.2 78.3 all-gather.15
  341.3 78.3 all-gather.17
  422.3 150.0 all-gather.21
  575.2 149.5 all-gather.19
  727.6 149.5 all-gather.23
  918.3 136.5 reduce-scatter.19
  1059.9 137.4 reduce-scatter.17
  1202.6 138.0 reduce-scatter.15
  1345.8 137.8 reduce-scatter.13
  1488.8 137.8 reduce-scatter.11
  1632.2 201.6 reduce-scatter.25
  1839.5 202.1 reduce-scatter.23
  2047.2 202.1 reduce-scatter.21
  2254.5 122.4 reduce-scatter.27
  2379.7 24.2 all-reduce.9
where the time goes:
time: 2430 us; the launch traced here: 2420 us
  waiting for transfers between devices  1940 us (80%)
  matrix products  243 us (10%)
  blocking collectives  166 us (7%)
  other arithmetic  30.7 us (1%)
    reduce_scatter x1, waiting for transfers between devices, local(): lax.psum_scatter(grad_up_w.astype(jnp.bfloat16), 'shard', scatter_dimensi...  208 us
    reduce_scatter x1, waiting for transfers between devices, local(): lax.psum_scatter(grad_gate_w.astype(jnp.bfloat16), 'shard', scatter_dimen...  208 us
    reduce_scatter x1, waiting for transfers between devices, local(): lax.psum_scatter(grad_down.astype(jnp.bfloat16), 'shard', scatter_dimensi...  207 us
    all_gather x1, waiting for transfers between devices, local(): up_part = lax.all_gather(w_up, 'shard', axis=0, tiled=True)  146 us
    reduce_scatter x1, waiting for transfers between devices, local(): lax.psum_scatter(grad_value_w.astype(jnp.bfloat16), 'shard', scatter_dime...  143 us
    reduce_scatter x1, waiting for transfers between devices, local(): lax.psum_scatter(grad_query_w.astype(jnp.bfloat16), 'shard', scatter_dime...  143 us
    reduce_scatter x1, waiting for transfers between devices, local(): lax.psum_scatter(grad_key_w.astype(jnp.bfloat16), 'shard', scatter_dimens...  143 us
    all_gather x1, waiting for transfers between devices, local(): gate_part = lax.all_gather(w_gate, 'shard', axis=0, tiled=True)  142 us
  transfers between devices with their start and end apart: 18, of which 16 were waited for; matrix products, arithmetic and copies ran while one was open for 10% of the time, Pallas kernels for 0%

commit v1 on v0

--- a/solution.py
+++ b/solution.py
@@ -88,8 +88,11 @@
     gain_part = lax.all_gather(attn_gain, "shard", axis=0, tiled=True)
     query_part = lax.all_gather(w_query, "shard", axis=0, tiled=True)
     key_part = lax.all_gather(w_key, "shard", axis=0, tiled=True)
-    value_part = lax.all_gather(w_value, "shard", axis=0, tiled=True)
-    outgate_part = lax.all_gather(w_outgate, "shard", axis=0, tiled=True)
+    value_part, outgate_part = jnp.split(
+        lax.all_gather(jnp.concatenate([w_value, w_outgate], axis=1), "shard", axis=0, tiled=True),
+        [w_value.shape[1]],
+        axis=1,
+    )
     forget_part = lax.all_gather(w_forget, "shard", axis=0, tiled=True)
     normed_part = (scaled1 * gain_part.astype(jnp.float32)).astype(jnp.bfloat16)
     gain_one = gain_part

time: 2430 us -> 2590 us (1.066)
  waiting for transfers between devices: 1940 us -> 2100 us
    reduce_scatter x1, waiting for transfers between devices: 0.01 us -> 143 us  [local(): lax.psum_scatter(grad_output_w.astype(jnp.bfloat16), 'shard', scatter_dim...]
    reduce_scatter x1, waiting for transfers between devices: 143 us -> 7.14 us  [local(): lax.psum_scatter(grad_query_w.astype(jnp.bfloat16), 'shard', scatter_dime...]
    all_gather x0 -> x1, waiting for transfers between devices: none -> 99.9 us  [local(): lax.all_gather(jnp.concatenate([w_value, w_outgate], axis=1), 'shard', ax...]
    reduce_scatter x1, waiting for transfers between devices: 110 us -> 143 us  [local(): lax.psum_scatter(grad_outgate_w.astype(jnp.bfloat16), 'shard', scatter_di...]
    all_gather x1, waiting for transfers between devices: 46.6 us -> 74.1 us  [local(): outgate_part = lax.all_gather(w_outgate, 'shard', axis=0, tiled=True)]
    unnamed x19 -> x20, waiting for transfers between devices: 62.1 us -> 66.4 us
  transfers between devices with their start and end apart: 18 -> 19, of which waited for: 16 -> 18; matrix products, arithmetic and copies ran while one was open for 10% -> 8% of each run, Pallas kernels for 0% -> 0%
where the time goes in v1:
time: 2590 us
  waiting for transfers between devices  2100 us (81%)
  matrix products  246 us (9%)
  blocking collectives  165 us (6%)
  other arithmetic  32 us (1%)
    reduce_scatter x1, waiting for transfers between devices, local(): lax.psum_scatter(grad_down.astype(jnp.bfloat16), 'shard', scatter_dimensi...  208 us
    reduce_scatter x1, waiting for transfers between devices, local(): lax.psum_scatter(grad_up_w.astype(jnp.bfloat16), 'shard', scatter_dimensi...  208 us
    reduce_scatter x1, waiting for transfers between devices, local(): lax.psum_scatter(grad_gate_w.astype(jnp.bfloat16), 'shard', scatter_dimen...  207 us
    all_gather x1, waiting for transfers between devices, local(): gate_part = lax.all_gather(w_gate, 'shard', axis=0, tiled=True)  146 us
    reduce_scatter x1, waiting for transfers between devices, local(): lax.psum_scatter(grad_outgate_w.astype(jnp.bfloat16), 'shard', scatter_di...  143 us
    reduce_scatter x1, waiting for transfers between devices, local(): lax.psum_scatter(grad_key_w.astype(jnp.bfloat16), 'shard', scatter_dimens...  143 us
    reduce_scatter x1, waiting for transfers between devices, local(): lax.psum_scatter(grad_value_w.astype(jnp.bfloat16), 'shard', scatter_dime...  143 us
    reduce_scatter x1, waiting for transfers between devices, local(): lax.psum_scatter(grad_output_w.astype(jnp.bfloat16), 'shard', scatter_dim...  143 us
  transfers between devices with their start and end apart: 19, of which 18 were waited for; matrix products, arithmetic and copies ran while one was open for 8% of the time, Pallas kernels for 0%

profile of v1, /device:TPU:0, one launch (start us, length us, event | category | flops | bytes accessed | tf_op | source)
XLA Modules:
  0.0 2585.5 jit_solution(6025729523362079208)
XLA Ops:
  15.1 45.3 %all-reduce.5 = (bf16[1536]{0:T(1024)(128)(2,1)S(1)}, bf16[1536]{0:T(1024)(128)(2,1)S(1)}) all-reduce(bf16[1536]{0:T(1024)(128)(2,1)S(1)} %dynamic-update-slice, bf16[1536]{0:T(1024)(128)(2,1)S(1)} %dynamic-update-slice.1), channel_id=1, replica_groups=mesh['rep'=2,'shard'=16] {'shard'}, use_global_device_ids=true, to_apply=%add | all-reduce | flops 3072 | bytes 12288
  60.5 37.2 %all-gather = bf16[16,96,24]{1,2,0:T(8,128)(2,1)S(1)} all-gather(bf16[1,96,24]{1,2,0:T(8,128)(2,1)S(1)} %bitcast.93), channel_id=1, replica_groups=mesh['rep'=2,'shard'=16] {'shard'}, dimensions={0}, use_global_device_ids=true | all-gather | bytes 78336 | tf_op jit(solution)/shard_map/all_gather | solution.py:96
  105.7 70.7 %all-gather.15.cloned.1.call-done = bf16[1536,1536]{1,0:T(8,128)(2,1)} async-done(((bf16[96,1536]{1,0:T(8,128)(2,1)}), bf16[1536,1536]{1,0:T(8,128)(2,1)}) %all-gather.15.cloned.1.call-update) | async-done | bytes 4718608 | tf_op jit(solution)/shard_map/all_gather | solution.py:90
  176.4 5.4 convolution_convert_fusion.8
  183.5 8.1 fusion.101
  191.7 7.4 fusion.4
  200.3 99.9 %all-gather.11.cloned.1.call-done = bf16[1536,3072]{1,0:T(8,128)(2,1)} async-done(((bf16[96,3072]{1,0:T(8,128)(2,1)}), bf16[1536,3072]{1,0:T(8,128)(2,1)}) %all-gather.11.cloned.1.call-update) | async-done | bytes 9437200 | tf_op jit(solution)/shard_map/all_gather | solution.py:92
  305.4 9.8 fusion.10
  317.4 7.3 multiply_convert_fusion.9
  324.7 56.2 %all-gather.17.cloned.1.call-done = bf16[1536,1536]{1,0:T(8,128)(2,1)} async-done(((bf16[96,1536]{1,0:T(8,128)(2,1)}), bf16[1536,1536]{1,0:T(8,128)(2,1)}) %all-gather.17.cloned.1.call-update) | async-done | bytes 4718608 | tf_op jit(solution)/shard_map/all_gather | solution.py:121
  380.9 4.8 multiply_reduce_fusion.3
  387.6 146.0 %all-gather.19.cloned.1.call-done = bf16[1536,4096]{1,0:T(8,128)(2,1)} async-done(((bf16[96,4096]{1,0:T(8,128)(2,1)}), bf16[1536,4096]{1,0:T(8,128)(2,1)}) %all-gather.19.cloned.1.call-update) | async-done | bytes 12582928 | tf_op jit(solution)/shard_map/all_gather | solution.py:125
  533.6 10.0 fusion.103
  543.6 142.3 %all-gather.21.cloned.1.call-done = bf16[1536,4096]{1,0:T(8,128)(2,1)} async-done(((bf16[96,4096]{1,0:T(8,128)(2,1)}), bf16[1536,4096]{1,0:T(8,128)(2,1)}) %all-gather.21.cloned.1.call-update) | async-done | bytes 12582928 | tf_op jit(solution)/shard_map/all_gather | solution.py:126
  685.9 10.0 fusion.104
  695.8 142.4 %all-gather.23.cloned.1.call-done = bf16[4096,1536]{1,0:T(8,128)(2,1)} async-done(((bf16[256,1536]{1,0:T(8,128)(2,1)}), bf16[4096,1536]{1,0:T(8,128)(2,1)}) %all-gather.23.cloned.1.call-update) | async-done | bytes 12582928 | tf_op jit(solution)/shard_map/all_gather | solution.py:133
  838.3 15.2 multiply_convert_fusion.1
  853.5 9.7 fusion.105
  863.3 9.3 multiply_reduce_fusion.1
  881.7 22.4 fusion.99
  904.1 6.6 fusion.45
  911.7 4.9 convolution_convert_fusion.7
  916.7 8.0 fusion.46
  930.3 8.1 fusion.47
  944.1 5.7 convolution_convert_fusion.4
  949.9 5.6 convolution_convert_fusion.3
  955.6 11.6 convolution_convert_fusion.2
  967.3 11.5 convolution_convert_fusion.1
  978.9 11.3 convolution_convert_fusion
  997.4 4.9 fusion.106
  1002.3 5.9 convolution_add_fusion.3
  1008.2 39.3 %psum.90 = f32[24]{0:T(128)} all-reduce(f32[24]{0:T(128)S(1)} %get-tuple-element.53), channel_id=1, replica_groups=mesh['rep'=2,'shard'=16] {'rep','shard'}, use_global_device_ids=true, to_apply=%region_25.26 | all-reduce | flops 24 | bytes 192 | tf_op jit(solution)/shard_map/psum | solution.py:191
  1047.5 7.1 reduce-scatter.12.cloned.1.call-done
  1054.7 143.3 %reduce-scatter.14.cloned.1.call-done = bf16[96,1536]{1,0:T(8,128)(2,1)} async-done(((bf16[1536,1536]{1,0:T(8,128)(2,1)}), bf16[96,1536]{1,0:T(8,128)(2,1)}) %reduce-scatter.14.cloned.1.call-update) | async-done | bytes 294928 | tf_op jit(solution)/shard_map/reduce_scatter | solution.py:224
  1197.9 143.0 %reduce-scatter.16.cloned.1.call-done = bf16[96,1536]{1,0:T(8,128)(2,1)} async-done(((bf16[1536,1536]{1,0:T(8,128)(2,1)}), bf16[96,1536]{1,0:T(8,128)(2,1)}) %reduce-scatter.16.cloned.1.call-update) | async-done | bytes 294928 | tf_op jit(solution)/shard_map/reduce_scatter | solution.py:227
  1341.0 143.4 %reduce-scatter.18.cloned.1.call-done = bf16[96,1536]{1,0:T(8,128)(2,1)} async-done(((bf16[1536,1536]{1,0:T(8,128)(2,1)}), bf16[96,1536]{1,0:T(8,128)(2,1)}) %reduce-scatter.18.cloned.1.call-update) | async-done | bytes 294928 | tf_op jit(solution)/shard_map/reduce_scatter | solution.py:230
  1484.4 142.9 %reduce-scatter.20.cloned.1.call-done = bf16[96,1536]{1,0:T(8,128)(2,1)} async-done(((bf16[1536,1536]{1,0:T(8,128)(2,1)}), bf16[96,1536]{1,0:T(8,128)(2,1)}) %reduce-scatter.20.cloned.1.call-update) | async-done | bytes 294928 | tf_op jit(solution)/shard_map/reduce_scatter | solution.py:236
  1627.3 207.4 %reduce-scatter.22.cloned.1.call-done = bf16[96,4096]{1,0:T(8,128)(2,1)} async-done(((bf16[1536,4096]{1,0:T(8,128)(2,1)}), bf16[96,4096]{1,0:T(8,128)(2,1)}) %reduce-scatter.22.cloned.1.call-update) | async-done | bytes 786448 | tf_op jit(solution)/shard_map/reduce_scatter | solution.py:153
  1834.7 207.7 %reduce-scatter.24.cloned.1.call-done = bf16[96,4096]{1,0:T(8,128)(2,1)} async-done(((bf16[1536,4096]{1,0:T(8,128)(2,1)}), bf16[96,4096]{1,0:T(8,128)(2,1)}) %reduce-scatter.24.cloned.1.call-update) | async-done | bytes 786448 | tf_op jit(solution)/shard_map/reduce_scatter | solution.py:156
  2042.4 207.9 %reduce-scatter.26.cloned.1.call-done = bf16[256,1536]{1,0:T(8,128)(2,1)} async-done(((bf16[4096,1536]{1,0:T(8,128)(2,1)}), bf16[256,1536]{1,0:T(8,128)(2,1)}) %reduce-scatter.26.cloned.1.call-update) | async-done | bytes 786448 | tf_op jit(solution)/shard_map/reduce_scatter | solution.py:159
  2250.3 81.8 %all-gather.25.cloned.1.call-done = bf16[1536,1536]{1,0:T(8,128)(2,1)} async-done(((bf16[96,1536]{1,0:T(8,128)(2,1)}), bf16[1536,1536]{1,0:T(8,128)(2,1)}) %all-gather.25.cloned.1.call-update) | async-done | bytes 4718608 | tf_op jit(solution)/shard_map/all_gather | solution.py:198
  2332.1 6.9 convolution_add_fusion.2
  2339.0 74.1 %all-gather.27.cloned.1.call-done = bf16[1536,1536]{1,0:T(8,128)(2,1)} async-done(((bf16[96,1536]{1,0:T(8,128)(2,1)}), bf16[1536,1536]{1,0:T(8,128)(2,1)}) %all-gather.27.cloned.1.call-update) | async-done | bytes 4718608 | tf_op jit(solution)/shard_map/all_gather | solution.py:199
  2413.2 5.5 convolution_add_fusion.1
  2421.5 41.0 %all-reduce.4 = (bf16[1536]{0:T(1024)(128)(2,1)}, bf16[1536]{0:T(1024)(128)(2,1)}) all-reduce(bf16[1536]{0:T(1024)(128)(2,1)S(1)} %get-tuple-element.18, bf16[1536]{0:T(1024)(128)(2,1)} %get-tuple-element.16), channel_id=2, replica_groups=mesh['rep'=2,'shard'=16] {'shard'}, use_global_device_ids=true, to_apply=%region_12.13.clone | all-reduce | flops 3072 | bytes 12288
  2469.1 9.3 fusion.29
  2478.4 61.5 %reduce-scatter.28.cloned.1.call-done = bf16[96,24]{1,0:T(8,128)(2,1)} async-done(((bf16[1536,24]{1,0:T(8,128)(2,1)}), bf16[96,24]{1,0:T(8,128)(2,1)}) %reduce-scatter.28.cloned.1.call-update) | async-done | bytes 4624
  2544.9 22.2 all-reduce.10.cloned.1.call-done
  (184 shorter events, 80.9 us)
Async XLA Ops:
  7.2 93.2 %all-gather.13.cloned.1.call-start = ((), (), s32[]{:S(2)}) async-start(), calls=%async_computation.10 | async-start | bytes 5013504 | tf_op jit(solution)/shard_map/all_gather | solution.py:89
  7.9 5.5 copy-start.32
  7.9 6.7 copy-start.36
  7.9 7.0 copy-start.37
  7.9 52.5 %copy-start.31 = (bf16[96,24]{0,1:T(8,128)(2,1)S(1)}, bf16[96,24]{0,1:T(8,128)(2,1)}, u32[]{:S(2)}) copy-start(bf16[96,24]{0,1:T(8,128)(2,1)} %param.24) | copy-start | bytes 13828
  8.0 168.4 %all-gather.15.cloned.1.call-start = ((), (), s32[]{:S(2)}) async-start(), calls=%async_computation.11 | async-start | bytes 5013504 | tf_op jit(solution)/shard_map/all_gather | solution.py:90
  8.7 89.2 %copy-start.38 = (bf16[24]{0:T(256)(128)(2,1)S(1)}, bf16[24]{0:T(256)(128)(2,1)}, u32[]{:S(2)}) copy-start(bf16[24]{0:T(256)(128)(2,1)} %param.25) | copy-start | bytes 148
  8.7 89.3 %copy-start.33 = (s32[1,4]{1,0:T(1,128)S(1)}, s32[1,4]{1,0:T(1,128)}, u32[]{:S(2)}) copy-start(s32[1,4]{1,0:T(1,128)} %param.17) | copy-start | bytes 52
  8.7 89.3 %copy-start.34 = (s32[1,4]{1,0:T(1,128)S(1)}, s32[1,4]{1,0:T(1,128)}, u32[]{:S(2)}) copy-start(s32[1,4]{1,0:T(1,128)} %param.18) | copy-start | bytes 52
  8.7 89.4 %copy-start = (bf16[384,1536]{1,0:T(8,128)(2,1)S(1)}, bf16[384,1536]{1,0:T(8,128)(2,1)}, u32[]{:S(2)}) copy-start(bf16[384,1536]{1,0:T(8,128)(2,1)} %param.16) | copy-start | bytes 3538948
  8.7 291.5 %all-gather.11.cloned.1.call-start = ((), (), s32[]{:S(2)}) async-start(), calls=%async_computation.9 | async-start | bytes 10027008 | tf_op jit(solution)/shard_map/all_gather | solution.py:92
  10.8 370.1 %all-gather.17.cloned.1.call-start = ((), (), s32[]{:S(2)}) async-start(), calls=%async_computation.12 | async-start | bytes 5013504 | tf_op jit(solution)/shard_map/all_gather | solution.py:121
  11.4 522.2 %all-gather.19.cloned.1.call-start = ((), (), s32[]{:S(2)}) async-start(), calls=%async_computation.13 | async-start | bytes 13369344 | tf_op jit(solution)/shard_map/all_gather | solution.py:125
  12.0 673.9 %all-gather.21.cloned.1.call-start = ((), (), s32[]{:S(2)}) async-start(), calls=%async_computation.14 | async-start | bytes 13369344 | tf_op jit(solution)/shard_map/all_gather | solution.py:126
  12.6 825.7 %all-gather.23.cloned.1.call-start = ((), (), s32[]{:S(2)}) async-start(), calls=%async_computation.15 | async-start | bytes 13369344 | tf_op jit(solution)/shard_map/all_gather | solution.py:133
  13.3 1041.3 %reduce-scatter.12.cloned.1.call-start = ((), (), s32[]{:S(2)}) async-start(), calls=%async_computation.18 | async-start | bytes 5013504 | tf_op jit(solution)/shard_map/reduce_scatter | solution.py:221
  105.7 77.8 %copy-start.5 = (bf16[384,1536]{0,1:T(8,128)(2,1)}, bf16[384,1536]{0,1:T(8,128)(2,1)S(1)}, u32[]{:S(2)}) copy-start(bf16[384,1536]{0,1:T(8,128)(2,1)S(1)} %copy.67) | copy-start | bytes 3538948
  183.5 8.2 copy-start.6
  191.7 7.4 copy-start.21
  191.7 108.6 %copy-start.27 = (f32[384]{0:T(512)S(1)}, f32[384]{0:T(512)}, u32[]{:S(2)}) copy-start(f32[384]{0:T(512)} %copy-done.26) | copy-start | bytes 4612
  305.3 9.8 copy-start.13
  317.4 7.3 copy-start.1
  385.7 477.6 %copy-start.3 = (f32[384,1536]{1,0:T(8,128)}, f32[384,1536]{1,0:T(8,128)S(1)}, u32[]{:S(2)}) copy-start(f32[384,1536]{1,0:T(8,128)S(1)} %get-tuple-element.49) | copy-start | bytes 7077892
  853.5 9.8 copy-start.30
  853.5 9.8 copy-start.40
  853.5 21.6 slice-start
  863.3 9.3 copy-start.8
  863.3 11.8 slice-start.1
  904.1 7.6 copy-start.28
  916.7 281.3 %reduce-scatter.14.cloned.1.call-start = ((), (), s32[]{:S(2)}) async-start(), calls=%async_computation.19 | async-start | bytes 5013504 | tf_op jit(solution)/shard_map/reduce_scatter | solution.py:224
  930.3 410.7 %reduce-scatter.16.cloned.1.call-start = ((), (), s32[]{:S(2)}) async-start(), calls=%async_computation.20 | async-start | bytes 5013504 | tf_op jit(solution)/shard_map/reduce_scatter | solution.py:227
  944.0 540.4 %reduce-scatter.18.cloned.1.call-start = ((), (), s32[]{:S(2)}) async-start(), calls=%async_computation.21 | async-start | bytes 5013504 | tf_op jit(solution)/shard_map/reduce_scatter | solution.py:230
  949.9 677.5 %reduce-scatter.20.cloned.1.call-start = ((), (), s32[]{:S(2)}) async-start(), calls=%async_computation.22 | async-start | bytes 5013504 | tf_op jit(solution)/shard_map/reduce_scatter | solution.py:236
  955.6 879.1 %reduce-scatter.22.cloned.1.call-start = ((), (), s32[]{:S(2)}) async-start(), calls=%async_computation.23 | async-start | bytes 13369344 | tf_op jit(solution)/shard_map/reduce_scatter | solution.py:153
  967.3 1075.1 %reduce-scatter.24.cloned.1.call-start = ((), (), s32[]{:S(2)}) async-start(), calls=%async_computation.24 | async-start | bytes 13369344 | tf_op jit(solution)/shard_map/reduce_scatter | solution.py:156
  978.8 1271.4 %reduce-scatter.26.cloned.1.call-start = ((), (), s32[]{:S(2)}) async-start(), calls=%async_computation.25 | async-start | bytes 13369344 | tf_op jit(solution)/shard_map/reduce_scatter | solution.py:159
  990.3 1341.9 %all-gather.25.cloned.1.call-start = ((), (), s32[]{:S(2)}) async-start(), calls=%async_computation.16 | async-start | bytes 5013504 | tf_op jit(solution)/shard_map/all_gather | solution.py:198
  990.8 1422.3 %all-gather.27.cloned.1.call-start = ((), (), s32[]{:S(2)}) async-start(), calls=%async_computation.17 | async-start | bytes 5013504 | tf_op jit(solution)/shard_map/all_gather | solution.py:199
  991.4 1548.5 %reduce-scatter.28.cloned.1.call-start = ((), (), s32[]{:S(2)}) async-start(), calls=%async_computation.26 | async-start | bytes 417792
  997.1 1570.0 %all-reduce.10.cloned.1.call-start = ((), (), s32[]{:S(2)}) async-start(), calls=%async_computation.27 | async-start | bytes 7667712 | tf_op jit(solution)/shard_map/psum | solution.py:242
  997.4 4.9 copy-start.12
  2413.2 5.5 copy-start.20
  2413.2 5.5 copy-start.25
  2469.1 71.6 %copy-start.35 = (bf16[96]{0:T(256)(128)(2,1)S(1)}, bf16[96]{0:T(256)(128)(2,1)}, u32[]{:S(2)}) copy-start(bf16[96]{0:T(256)(128)(2,1)} %dynamic-slice.5) | copy-start | bytes 580
  2567.1 5.7 copy-start.18
  2567.1 6.5 copy-start.17
  2567.1 7.4 copy-start.16
  2570.9 4.9 copy-start.15
  (15 other events, 26.8 us)
Sparse Core Ops, SparseCore 0:
  10.8 83.7 all-gather.12
  97.4 78.9 all-gather.14
  179.8 120.3 all-gather.10
  302.9 77.9 all-gather.16
  383.5 150.0 all-gather.18
  536.2 149.5 all-gather.20
  688.6 149.5 all-gather.22
  916.8 137.8 reduce-scatter.11
  1059.8 138.0 reduce-scatter.13
  1203.0 137.9 reduce-scatter.15
  1346.1 138.2 reduce-scatter.17
  1489.4 137.8 reduce-scatter.19
  1633.0 201.6 reduce-scatter.21
  1840.2 202.1 reduce-scatter.23
  2047.9 202.3 reduce-scatter.25
  2252.9 79.1 all-gather.24
  2334.8 78.3 all-gather.26
  2418.3 121.6 reduce-scatter.27
  2542.8 24.2 all-reduce.9
